TPU v7x, 128 devices: a whole 4x4x4 slice. The times are simulated.
128 devices in a mesh: slab: 64 (over z, y, x), sub: 2 (over core).
Axes of the slice: x: 4, y: 4, z: 4, core: 2. Of those that a mesh axis runs over, the one named last changes fastest.
Arguments:
- part_cells: int32 [128, 128, 256], P(('slab', 'sub')), may hold values from 0 to 8191
- part_offsets: float32 [128, 128, 3, 256], P(('slab', 'sub')), may hold values from 0 to 1
- part_counts: int32 [128, 128], P(('slab', 'sub')), may hold values from 32 to 256, as said below
- w_first: bfloat16 [16, 27], replicated, may hold values from -1.25 to 1.25
- w_mid: bfloat16 [16, 432], replicated, may hold values from -0.3125 to 0.3125
- w_last: bfloat16 [16, 432], replicated, may hold values from -0.3125 to 0.3125
- w_head: bfloat16 [3, 32], replicated, may hold values from -1 to 1
- cotangent: bfloat16 [3, 256, 16, 256], P(None, 'slab', 'sub'), may hold values from -6 to 6
Outputs:
- force: bfloat16 [3, 256, 16, 256], P(None, 'slab', 'sub')
- grad_first: float32 [16, 27], replicated
- grad_mid: float32 [16, 432], replicated
- grad_last: float32 [16, 432], replicated
- grad_head: float32 [3, 32], replicated
Inputs may be any that keep to these rules, and one draw needn't show every extreme that they name: part_counts[s, d] is the number of used slots among the 256 slots from device s to brick d; one brick, drawn from the seed, gets 256 from every device. part_cells[s, d, k] is the cell (i * 8 + j) * 256 + l in brick d's own cells; slots at or above part_counts[s, d] are unused.
All inputs are finite; a program needn't handle non-finite values.
Results may differ from a plain program's by a relative error of at most 0.003.
The roundings to bfloat16 on the way count: a program that leaves them out, or rounds other values in their place, can miss the bound.
Values may be sent and summed in bfloat16 or wider, within the bound.
A program may use at most 192 MiB of HBM per device.

v0:
```python
import math
import jax
import jax.numpy as jnp
from jax import lax
from jax.sharding import PartitionSpec as P


def padded_2(x, sides, width):
    for axis, dim in sides:
        devices, length = (lax.axis_size(axis), x.shape[dim])
        up = [(i, (i + 1) % devices) for i in range(devices)]
        down = [(j, i) for i, j in up]
        last = lax.slice_in_dim(x, length - width, length, axis=dim)
        initial = lax.slice_in_dim(x, 0, width, axis=dim)
        before = lax.ppermute(last, axis, up)
        after = lax.ppermute(initial, axis, down)
        x = jnp.concatenate([before, x, after], axis=dim)
    return x


def passed_along(x, axis, by):
    devices = lax.axis_size(axis)
    return lax.ppermute(x, axis, [(i, (i + by) % devices) for i in range(devices)])


def silu_slope(value):
    sigma = jax.nn.sigmoid(value)
    return sigma * (1.0 + value * (1.0 - sigma))


def z_stack(plane):
    return jnp.concatenate([jnp.roll(plane, 1, axis=2), plane, jnp.roll(plane, -1, axis=2)], 0)


def conv_planes(padded, kernel, stacker):
    chans = padded.shape[0]
    out_x = padded.shape[1] - 2
    out_y = padded.shape[2] - 2
    out_chans = kernel.shape[0]
    blocks = kernel.reshape(out_chans, 3, 3, 3 * chans)
    stacks = [stacker(padded[:, plane]) for plane in range(out_x + 2)]
    depth_z = stacks[0].shape[2]
    results = []
    for plane in range(out_x):
        total = jnp.zeros((out_chans, out_y * depth_z), jnp.float32)
        for shift_x in range(3):
            for shift_y in range(3):
                piece = stacks[plane + shift_x][:, shift_y : shift_y + out_y].reshape(
                    3 * chans, out_y * depth_z
                )
                total = total + jnp.dot(
                    blocks[:, shift_x, shift_y], piece, preferred_element_type=jnp.float32
                )
        results.append(total.reshape(out_chans, out_y, depth_z))
    return jnp.stack(results, 1)


def weight_grad(padded, grad, stacker):
    chans = padded.shape[0]
    out_x = grad.shape[1]
    out_y = grad.shape[2]
    depth_z = grad.shape[3]
    out_chans = grad.shape[0]
    totals = [
        [jnp.zeros((out_chans, 3 * chans), jnp.float32) for shift_y in range(3)]
        for shift_x in range(3)
    ]
    for plane in range(out_x):
        grad_plane = grad[:, plane].reshape(out_chans, out_y * depth_z)
        for shift_x in range(3):
            stacked = stacker(padded[:, plane + shift_x])
            for shift_y in range(3):
                piece = stacked[:, shift_y : shift_y + out_y].reshape(3 * chans, out_y * depth_z)
                totals[shift_x][shift_y] = totals[shift_x][shift_y] + lax.dot_general(
                    grad_plane, piece, (((1,), (1,)), ((), ())), preferred_element_type=jnp.float32
                )
    joined = jnp.stack([jnp.stack(totals[shift_x], axis=1) for shift_x in range(3)], axis=1)
    return joined.reshape(out_chans, 27 * chans)


def flip_kernel(weights, chans):
    out_chans = weights.shape[0]
    shaped = weights.reshape(out_chans, 3, 3, 3, chans)[:, ::-1, ::-1, ::-1, :]
    return shaped.transpose(4, 1, 2, 3, 0).reshape(chans, 27 * out_chans)


def with_rims(field):
    return padded_2(field, (("slab", 1), ("sub", 2)), 1)


def finish(
    density_rim,
    pre_one,
    hidden_one,
    hidden_one_rim,
    pre_two,
    hidden_two_rim,
    w_mid,
    w_last,
    w_head,
    ct_field,
    rims,
    stacker,
):
    channels = w_mid.shape[0]
    extent = pre_one.shape[1:]
    pre_three = conv_planes(hidden_two_rim, w_last, stacker)
    hidden_three = jax.nn.silu(pre_three).astype(jnp.bfloat16)
    features = jnp.concatenate([hidden_three, hidden_one], 0).reshape(2 * channels, -1)
    ct_flat = ct_field.reshape(3, -1)
    force = jnp.dot(w_head, features, preferred_element_type=jnp.float32).astype(jnp.bfloat16)
    force = force.reshape((3,) + extent)
    grad_head = lax.dot_general(
        ct_flat, features, (((1,), (1,)), ((), ())), preferred_element_type=jnp.float32
    )
    back_features = jnp.dot(w_head.T, ct_flat, preferred_element_type=jnp.float32)
    grad_three = (back_features[:channels] * silu_slope(pre_three.reshape(channels, -1))).astype(
        jnp.bfloat16
    )
    grad_three = grad_three.reshape((channels,) + extent)
    grad_last = weight_grad(hidden_two_rim, grad_three, stacker)
    back_two = conv_planes(rims(grad_three), flip_kernel(w_last, channels), stacker)
    grad_two = (back_two * silu_slope(pre_two)).astype(jnp.bfloat16)
    grad_mid = weight_grad(hidden_one_rim, grad_two, stacker)
    back_one = conv_planes(rims(grad_two), flip_kernel(w_mid, channels), stacker)
    back_one = back_one + back_features[channels:].reshape((channels,) + extent)
    grad_one = (back_one * silu_slope(pre_one)).astype(jnp.bfloat16)
    grad_first = weight_grad(density_rim, grad_one, stacker)
    return (force, grad_first, grad_mid, grad_last, grad_head)


def per_device(part_cells, part_offsets, part_counts, w_first, w_mid, w_last, w_head, cotangent):
    n_slab = lax.axis_size("slab")
    n_sub = lax.axis_size("sub")
    width_x = cotangent.shape[1]
    width_y = cotangent.shape[2]
    depth_z = cotangent.shape[3]
    slot_cap = part_cells.shape[2]
    got_cells, got_offsets, got_counts = (
        lax.all_to_all(part_cells, ("slab", "sub"), split_axis=1, concat_axis=0, tiled=True),
        lax.all_to_all(part_offsets, ("slab", "sub"), split_axis=1, concat_axis=0, tiled=True),
        lax.all_to_all(part_counts, ("slab", "sub"), split_axis=1, concat_axis=0, tiled=True),
    )
    slot_cells = got_cells.reshape(-1, slot_cap)
    offsets = got_offsets.reshape(-1, 3, slot_cap)
    counts = got_counts.reshape(-1)
    slot_ids = jnp.arange(slot_cap, dtype=jnp.int32)
    live = (slot_ids[None, :] < counts[:, None]).astype(jnp.float32)
    cell_x = slot_cells // (width_y * depth_z)
    cell_y = slot_cells // depth_z % width_y
    cell_z = slot_cells % depth_z
    frac_x = offsets[:, 0]
    frac_y = offsets[:, 1]
    frac_z = offsets[:, 2]
    padded = jnp.zeros(((width_x + 1) * (width_y + 1) * depth_z,), jnp.float32)
    for corner_x in (0, 1):
        weight_x = frac_x if corner_x else 1.0 - frac_x
        for corner_y in (0, 1):
            weight_y = frac_y if corner_y else 1.0 - frac_y
            for corner_z in (0, 1):
                weight_z = frac_z if corner_z else 1.0 - frac_z
                share = live * weight_x * weight_y * weight_z
                index = ((cell_x + corner_x) * (width_y + 1) + cell_y + corner_y) * depth_z + (
                    cell_z + corner_z
                ) % depth_z
                padded = padded.at[index.reshape(-1)].add(share.reshape(-1))
    padded = padded.reshape(width_x + 1, width_y + 1, depth_z)
    from_below = passed_along(padded[width_x], "slab", 1)
    core = padded[:width_x].at[0].add(from_below)
    from_side = passed_along(core[:, width_y], "sub", 1)
    density = core[:, :width_y].at[:, 0].add(from_side)
    density_b = density.astype(jnp.bfloat16)[None]
    density_rim = with_rims(density_b)
    pre_one = conv_planes(density_rim, w_first, z_stack)
    hidden_one = jax.nn.silu(pre_one).astype(jnp.bfloat16)
    hidden_one_rim = with_rims(hidden_one)
    pre_two = conv_planes(hidden_one_rim, w_mid, z_stack)
    hidden_two = jax.nn.silu(pre_two).astype(jnp.bfloat16)
    hidden_two_rim = with_rims(hidden_two)
    force, grad_first, grad_mid, grad_last, grad_head = finish(
        density_rim,
        pre_one,
        hidden_one,
        hidden_one_rim,
        pre_two,
        hidden_two_rim,
        w_mid,
        w_last,
        w_head,
        cotangent,
        with_rims,
        z_stack,
    )
    sum_first, sum_mid, sum_last, sum_head = lax.psum(
        (grad_first, grad_mid, grad_last, grad_head), ("slab", "sub")
    )
    loss_scale = 1.0 / math.sqrt(width_x * n_slab * width_y * n_sub * depth_z)
    return (
        force,
        loss_scale * sum_first,
        loss_scale * sum_mid,
        loss_scale * sum_last,
        loss_scale * sum_head,
    )


def solution(mesh):
    in_specs = (
        P(("slab", "sub"), None, None),
        P(("slab", "sub"), None, None, None),
        P(("slab", "sub"), None),
        P(),
        P(),
        P(),
        P(),
        P(None, "slab", "sub", None),
    )
    out_specs = (P(None, "slab", "sub", None), P(), P(), P(), P())
    return jax.shard_map(
        per_device, mesh=mesh, in_specs=in_specs, out_specs=out_specs, check_vma=False
    )
```

profile of v0, /device:TPU:1, one launch (start us, length us, event | category | flops | bytes accessed | tf_op | source)
XLA Modules:
  0.0 1670.1 jit_solution(12769515616592546914)
XLA Ops:
  0.6 1.4 copy.241
  2.0 11.5 all-to-all-start.1
  13.5 1.7 copy.240
  15.2 2.1 copy.242
  17.3 5.9 all-to-all-done.1
  23.1 4.5 all-to-all-start
  27.6 2.4 reduce.4
  30.1 7.5 all-to-all-done
  37.7 4.2 all-to-all-start.2
  41.9 3.0 compare_select_fusion
  44.9 1.8 compare_select_fusion.1
  46.6 1.3 compare_select_fusion.5
  47.9 7.6 all-to-all-done.2
  55.9 0.9 fusion.42
  56.8 171.0 %scatter_custom_fusion = f32[11520]{0:T(1024)S(1)} fusion(s32[32768]{0:T(1024)S(1)} %bitcast.1767, f32[32768]{0:T(1024)S(1)} %get-tuple-element.95, f32[]{:T(128)} %constant.137.clone.1), kind=kCustom, calls=%fused_computation.492 | custom fusion | flops 32768 | bytes 46084 | tf_op jit(solution)/shard_map/scatter-add | solution.py:166
  227.8 174.7 %scatter_fusion = f32[11520]{0:T(1024)S(1)} fusion(f32[11520]{0:T(1024)S(1)} %scatter_custom_fusion, s32[32768]{0:T(1024)S(1)} %bitcast.1646, f32[32768]{0:T(1024)S(1)} %get-tuple-element.94), kind=kCustom, calls=%fused_computation.1 | custom fusion | flops 32768 | bytes 524288 | tf_op jit(solution)/shard_map/scatter-add | solution.py:166
  402.5 174.9 %scatter_fusion.1 = f32[11520]{0:T(1024)S(1)} fusion(f32[11520]{0:T(1024)S(1)} %scatter_fusion, s32[32768]{0:T(1024)S(1)} %bitcast.1645, f32[32768]{0:T(1024)S(1)} %get-tuple-element.89), kind=kCustom, calls=%fused_computation.2 | custom fusion | flops 32768 | bytes 524288 | tf_op jit(solution)/shard_map/scatter-add | solution.py:166
  577.4 174.7 %scatter_fusion.2 = f32[11520]{0:T(1024)S(1)} fusion(f32[11520]{0:T(1024)S(1)} %scatter_fusion.1, s32[32768]{0:T(1024)S(1)} %bitcast.1643, f32[32768]{0:T(1024)S(1)} %copy-done.25), kind=kCustom, calls=%fused_computation.3 | custom fusion | flops 32768 | bytes 524288 | tf_op jit(solution)/shard_map/scatter-add | solution.py:166
  752.2 174.7 %scatter_fusion.3 = f32[11520]{0:T(1024)S(1)} fusion(f32[11520]{0:T(1024)S(1)} %scatter_fusion.2, s32[32768]{0:T(1024)S(1)} %bitcast.1644, f32[32768]{0:T(1024)S(1)} %copy-done.24), kind=kCustom, calls=%fused_computation.4 | custom fusion | flops 32768 | bytes 524288 | tf_op jit(solution)/shard_map/scatter-add | solution.py:166
  926.9 174.7 %scatter_fusion.4 = f32[11520]{0:T(1024)S(1)} fusion(f32[11520]{0:T(1024)S(1)} %scatter_fusion.3, s32[32768]{0:T(1024)S(1)} %bitcast.1642, f32[32768]{0:T(1024)S(1)} %copy-done.23), kind=kCustom, calls=%fused_computation.5 | custom fusion | flops 32768 | bytes 524288 | tf_op jit(solution)/shard_map/scatter-add | solution.py:166
  1101.7 174.7 %scatter_fusion.5 = f32[11520]{0:T(1024)S(1)} fusion(f32[11520]{0:T(1024)S(1)} %scatter_fusion.4, s32[32768]{0:T(1024)S(1)} %bitcast.1641, f32[32768]{0:T(1024)S(1)} %copy-done.22), kind=kCustom, calls=%fused_computation.6 | custom fusion | flops 32768 | bytes 524288 | tf_op jit(solution)/shard_map/scatter-add | solution.py:166
  1276.4 174.7 %scatter_fusion.6 = f32[11520]{0:T(1024)S(1)} fusion(f32[11520]{0:T(1024)S(1)} %scatter_fusion.5, s32[32768]{0:T(1024)S(1)} %bitcast.1640, f32[32768]{0:T(1024)S(1)} %copy-done.21), kind=kCustom, calls=%fused_computation.7 | custom fusion | flops 32768 | bytes 524288 | tf_op jit(solution)/shard_map/scatter-add | solution.py:166
  1451.3 8.0 collective-permute-done
  1459.3 2.1 collective-permute-start.1
  1462.4 6.9 collective-permute-start.3
  1469.3 1.0 collective-permute-done.2
  1470.3 1.6 collective-permute-start.4
  1483.7 7.2 collective-permute-start.7
  1491.0 1.3 fusion.221
  1492.4 0.9 collective-permute-done.6
  1506.3 7.0 collective-permute-start.11
  1520.2 1.8 rev.7
  1522.0 1.8 copy.302
  1523.8 1.0 reshape_reshape.7
  1524.8 1.8 rev.6
  1526.7 1.8 copy.296
  1528.4 1.0 reshape_reshape.6
  1532.4 1.0 pad_maximum_fusion.2
  1543.2 1.0 copy-done.1
  1546.0 1.6 collective-permute-start.15
  1552.9 3.6 collective-permute-done.14
  1557.4 1.6 collective-permute-start.16
  1559.8 1.0 copy.473
  1560.9 1.5 pad_maximum_fusion
  1575.0 2.5 collective-permute-start.19
  1582.4 3.7 collective-permute-done.18
  1586.1 2.0 collective-permute-start.20
  1604.5 62.7 %all-reduce = (f32[16,27]{0,1:T(8,128)S(1)}, f32[16,432]{1,0:T(8,128)S(1)}, f32[16,432]{1,0:T(8,128)S(1)}, f32[3,32]{1,0:T(4,128)S(1)}) all-reduce(f32[16,27]{0,1:T(8,128)S(1)} %reshape.1267, f32[16,432]{1,0:T(8,128)S(1)} %reshape.1268, f32[16,432]{1,0:T(8,128)S(1)} %reshape.1269, ...), channel_id=1, replica_groups=mesh['slab'=64,'sub'=2] {'slab','sub'}, use_global_device_ids=true, to_apply=%region_8.9 | all-reduce | flops 14352 | bytes 114816 | tf_op jit(solution)/shard_map/psum | solution.py:194
  (818 shorter events, 88.7 us)
Async XLA Ops:
  0.6 1490.3 %copy-start = (bf16[3,32]{1,0:T(4,128)(2,1)S(1)}, bf16[3,32]{1,0:T(4,128)(2,1)}, u32[]{:S(2)}) copy-start(bf16[3,32]{1,0:T(4,128)(2,1)} %param.18) | copy-start | bytes 580
  2.0 21.1 %all-to-all-start.1 = ((s32[1,128,1]{2,0,1:T(1,128)}), s32[1,128,1]{2,0,1:T(1,128)S(1)}, u32[]{:S(2)}, u32[]{:S(2)}) async-start(s32[1,128,1]{2,0,1:T(1,128)} %copy.241), calls=%async_computation.1 | async-start | bytes 131072 | tf_op jit(solution)/shard_map/all_to_all | solution.py:142
  23.1 14.5 all-to-all-start
  37.7 17.9 %all-to-all-start.2 = ((f32[1,128,3,256]{3,2,0,1:T(4,128)}), f32[1,128,3,256]{3,2,0,1:T(4,128)S(1)}, u32[]{:S(2)}, u32[]{:S(2)}) async-start(f32[1,128,3,256]{3,2,0,1:T(4,128)} %copy.242), calls=%async_computation.2 | async-start | bytes 1048576 | tf_op jit(solution)/shard_map/all_to_all | solution.py:141
  402.5 174.9 %copy-start.20 = (s32[32768,1]{0,1:T(1,128)S(1)}, s32[32768,1]{0,1:T(1,128)}, u32[]{:S(2)}) copy-start(s32[32768,1]{0,1:T(1,128)} %get-tuple-element.367) | copy-start | bytes 393220
  402.5 174.9 %copy-start.25 = (f32[32768]{0:T(1024)S(1)}, f32[32768]{0:T(1024)}, u32[]{:S(2)}) copy-start(f32[32768]{0:T(1024)} %get-tuple-element.93) | copy-start | bytes 393220
  577.4 174.7 %copy-start.24 = (f32[32768]{0:T(1024)S(1)}, f32[32768]{0:T(1024)}, u32[]{:S(2)}) copy-start(f32[32768]{0:T(1024)} %get-tuple-element.90) | copy-start | bytes 393220
  577.4 174.7 %copy-start.26 = (s32[32768,1]{0,1:T(1,128)S(1)}, s32[32768,1]{0,1:T(1,128)}, u32[]{:S(2)}) copy-start(s32[32768,1]{0,1:T(1,128)} %get-tuple-element.219) | copy-start | bytes 393220
  752.2 174.7 %copy-start.19 = (s32[32768,1]{0,1:T(1,128)S(1)}, s32[32768,1]{0,1:T(1,128)}, u32[]{:S(2)}) copy-start(s32[32768,1]{0,1:T(1,128)} %get-tuple-element.218) | copy-start | bytes 393220
  752.2 174.7 %copy-start.23 = (f32[32768]{0:T(1024)S(1)}, f32[32768]{0:T(1024)}, u32[]{:S(2)}) copy-start(f32[32768]{0:T(1024)} %get-tuple-element.92) | copy-start | bytes 393220
  926.9 174.7 %copy-start.18 = (s32[32768,1]{0,1:T(1,128)S(1)}, s32[32768,1]{0,1:T(1,128)}, u32[]{:S(2)}) copy-start(s32[32768,1]{0,1:T(1,128)} %get-tuple-element.54) | copy-start | bytes 393220
  926.9 174.7 %copy-start.22 = (f32[32768]{0:T(1024)S(1)}, f32[32768]{0:T(1024)}, u32[]{:S(2)}) copy-start(f32[32768]{0:T(1024)} %get-tuple-element.91) | copy-start | bytes 393220
  1101.7 174.7 %copy-start.17 = (s32[32768,1]{0,1:T(1,128)S(1)}, s32[32768,1]{0,1:T(1,128)}, u32[]{:S(2)}) copy-start(s32[32768,1]{0,1:T(1,128)} %get-tuple-element.48) | copy-start | bytes 393220
  1101.7 174.7 %copy-start.21 = (f32[32768]{0:T(1024)S(1)}, f32[32768]{0:T(1024)}, u32[]{:S(2)}) copy-start(f32[32768]{0:T(1024)} %get-tuple-element.88) | copy-start | bytes 393220
  1276.4 195.9 %copy-start.69 = (bf16[16,27]{1,0:T(8,128)(2,1)S(1)}, bf16[16,27]{1,0:T(8,128)(2,1)}, u32[]{:S(2)}) copy-start(bf16[16,27]{1,0:T(8,128)(2,1)} %param.15) | copy-start | bytes 2596
  1276.4 196.0 %copy-start.67 = (bf16[3,4,8,256]{3,2,1,0:T(8,128)(2,1)S(1)}, bf16[3,4,8,256]{3,2,1,0:T(8,128)(2,1)}, u32[]{:S(2)}) copy-start(bf16[3,4,8,256]{3,2,1,0:T(8,128)(2,1)} %param.19) | copy-start | bytes 147460
  1451.2 8.1 collective-permute-start
  1459.3 2.9 collective-permute-start.1
  1462.3 8.0 collective-permute-start.2
  1462.4 7.9 collective-permute-start.3
  1470.3 2.4 collective-permute-start.4
  1471.8 1.6 collective-permute-start.5
  1474.5 8.5 copy-start.51
  1474.5 8.3 copy-start.53
  1474.5 8.0 copy-start.55
  1474.6 7.7 copy-start.37
  1474.7 7.5 copy-start.39
  1474.7 7.2 copy-start.41
  1483.5 8.9 copy-start.63
  1483.6 10.7 copy-start.65
  1483.7 9.6 collective-permute-start.6
  1483.7 9.6 collective-permute-start.7
  1493.3 1.6 collective-permute-start.8
  1494.0 1.2 collective-permute-start.9
  1504.5 9.4 copy-start.64
  1504.5 10.2 copy-start.66
  1506.3 23.2 %collective-permute-start.10 = (bf16[16,1,8,256]{3,0,2,1:T(8,128)(2,1)}, bf16[16,1,8,256]{3,0,2,1:T(8,128)(2,1)}, u32[]{:S(2)}, u32[]{:S(2)}) collective-permute-start(bf16[16,1,8,256]{3,0,2,1:T(8,128)(2,1)} %get-tuple-element.134), channel_id=1, source_target_pairs={{0,2},{2,4},{4,6},{6,8},{8,10},{10,12},{12,14},{14,16},{16,18},{18... | collective-permute-start | bytes 196616 | tf_op jit(solution)/shard_map/ppermute | solution.py:15
  1506.3 23.2 %collective-permute-start.11 = (bf16[16,1,8,256]{3,0,2,1:T(8,128)(2,1)}, bf16[16,1,8,256]{3,0,2,1:T(8,128)(2,1)}, u32[]{:S(2)}, u32[]{:S(2)}) collective-permute-start(bf16[16,1,8,256]{3,0,2,1:T(8,128)(2,1)} %get-tuple-element.135), channel_id=1, source_target_pairs={{2,0},{4,2},{6,4},{8,6},{10,8},{12,10},{14,12},{16,14},{18,16},{20... | collective-permute-start | bytes 196616 | tf_op jit(solution)/shard_map/ppermute | solution.py:16
  1530.3 1.6 collective-permute-start.12
  1531.0 1.4 collective-permute-start.13
  1546.0 10.5 collective-permute-start.15
  1547.9 8.6 collective-permute-start.14
  1557.4 3.5 collective-permute-start.16
  1559.0 2.0 collective-permute-start.17
  1575.0 7.4 collective-permute-start.19
  1577.5 8.6 collective-permute-start.18
  1586.1 2.9 collective-permute-start.20
  1588.1 1.5 collective-permute-start.21
  (47 other events, 90.7 us)
where the time goes:
time: 1680 us; the launch traced here: 1670 us
  other arithmetic  1410 us (84%)
  blocking collectives  62.7 us (4%)
  starting transfers between devices  55.8 us (3%)
  matrix products  48.5 us (3%)
  waiting for transfers between devices  42.6 us (3%)
  local copies, waits for them, and re-layouts  42.4 us (3%)
    scatter-add x8, other arithmetic, per_device(): padded = padded.at[index.reshape(-1)].add(share.reshape(-1))  1390 us
    psum x1, blocking collectives, per_device(): lax.psum((grad_first, grad_mid, grad_last, grad_head), ('slab', 'sub'))  62.7 us
  transfers between devices with their start and end apart: 25, of which 17 were waited for; matrix products, arithmetic and copies ran while one was open for 3% of the time, Pallas kernels for 0%

commit v1 on v0

--- a/solution.py
+++ b/solution.py
@@ -3,6 +3,11 @@
 import jax.numpy as jnp
 from jax import lax
 from jax.sharding import PartitionSpec as P
+
+
+def one_after_other(array, axis_one, axis_two):
+    partial = lax.psum(array, axis_one)
+    return lax.psum(partial, axis_two)
 
 
 def padded_2(x, sides, width):
@@ -191,8 +196,8 @@
         with_rims,
         z_stack,
     )
-    sum_first, sum_mid, sum_last, sum_head = lax.psum(
-        (grad_first, grad_mid, grad_last, grad_head), ("slab", "sub")
+    sum_first, sum_mid, sum_last, sum_head = one_after_other(
+        (grad_first, grad_mid, grad_last, grad_head), "sub", "slab"
     )
     loss_scale = 1.0 / math.sqrt(width_x * n_slab * width_y * n_sub * depth_z)
     return (

time: 1680 us -> 1960 us (1.17)
  the two profiles are of different devices: /device:TPU:1 before, /device:TPU:0 now
where the time goes in v1:
time: 1960 us; the launch traced here: 1950 us
  other arithmetic  1410 us (72%)
  blocking collectives  348 us (18%)
  starting transfers between devices  52.8 us (3%)
  matrix products  48.5 us (2%)
  waiting for transfers between devices  44.3 us (2%)
  local copies, waits for them, and re-layouts  42.4 us (2%)
    scatter-add x8, other arithmetic, per_device(): padded = padded.at[index.reshape(-1)].add(share.reshape(-1))  1390 us
    psum x1, blocking collectives, one_after_other(): return lax.psum(partial, axis_two)  344 us
  transfers between devices with their start and end apart: 25, of which 17 were waited for; matrix products, arithmetic and copies ran while one was open for 2% of the time, Pallas kernels for 0%

profile of v1, /device:TPU:0, one launch (start us, length us, event | category | flops | bytes accessed | tf_op | source)
XLA Modules:
  0.0 1954.2 jit_solution(7304304142221128079)
XLA Ops:
  0.6 1.4 copy.241
  2.0 11.1 all-to-all-start.1
  13.2 1.7 copy.240
  14.9 2.1 copy.242
  16.9 5.6 all-to-all-done.1
  22.5 4.8 all-to-all-start
  27.3 2.4 reduce.4
  29.8 6.9 all-to-all-done
  36.7 4.8 all-to-all-start.2
  41.5 3.0 compare_select_fusion
  44.5 1.8 compare_select_fusion.1
  46.3 1.3 compare_select_fusion.5
  47.6 7.4 all-to-all-done.2
  55.3 0.9 fusion.42
  56.3 171.0 %scatter_custom_fusion = f32[11520]{0:T(1024)S(1)} fusion(s32[32768]{0:T(1024)S(1)} %bitcast.1767, f32[32768]{0:T(1024)S(1)} %get-tuple-element.99, f32[]{:T(128)} %constant.137.clone.1), kind=kCustom, calls=%fused_computation.492 | custom fusion | flops 32768 | bytes 46084 | tf_op jit(solution)/shard_map/scatter-add | solution.py:171
  227.2 174.7 %scatter_fusion = f32[11520]{0:T(1024)S(1)} fusion(f32[11520]{0:T(1024)S(1)} %scatter_custom_fusion, s32[32768]{0:T(1024)S(1)} %bitcast.1646, f32[32768]{0:T(1024)S(1)} %get-tuple-element.98), kind=kCustom, calls=%fused_computation.1 | custom fusion | flops 32768 | bytes 524288 | tf_op jit(solution)/shard_map/scatter-add | solution.py:171
  402.0 174.9 %scatter_fusion.1 = f32[11520]{0:T(1024)S(1)} fusion(f32[11520]{0:T(1024)S(1)} %scatter_fusion, s32[32768]{0:T(1024)S(1)} %bitcast.1645, f32[32768]{0:T(1024)S(1)} %get-tuple-element.93), kind=kCustom, calls=%fused_computation.2 | custom fusion | flops 32768 | bytes 524288 | tf_op jit(solution)/shard_map/scatter-add | solution.py:171
  576.9 174.7 %scatter_fusion.2 = f32[11520]{0:T(1024)S(1)} fusion(f32[11520]{0:T(1024)S(1)} %scatter_fusion.1, s32[32768]{0:T(1024)S(1)} %bitcast.1643, f32[32768]{0:T(1024)S(1)} %copy-done.25), kind=kCustom, calls=%fused_computation.3 | custom fusion | flops 32768 | bytes 524288 | tf_op jit(solution)/shard_map/scatter-add | solution.py:171
  751.7 174.7 %scatter_fusion.3 = f32[11520]{0:T(1024)S(1)} fusion(f32[11520]{0:T(1024)S(1)} %scatter_fusion.2, s32[32768]{0:T(1024)S(1)} %bitcast.1644, f32[32768]{0:T(1024)S(1)} %copy-done.24), kind=kCustom, calls=%fused_computation.4 | custom fusion | flops 32768 | bytes 524288 | tf_op jit(solution)/shard_map/scatter-add | solution.py:171
  926.4 174.7 %scatter_fusion.4 = f32[11520]{0:T(1024)S(1)} fusion(f32[11520]{0:T(1024)S(1)} %scatter_fusion.3, s32[32768]{0:T(1024)S(1)} %bitcast.1642, f32[32768]{0:T(1024)S(1)} %copy-done.23), kind=kCustom, calls=%fused_computation.5 | custom fusion | flops 32768 | bytes 524288 | tf_op jit(solution)/shard_map/scatter-add | solution.py:171
  1101.2 174.7 %scatter_fusion.5 = f32[11520]{0:T(1024)S(1)} fusion(f32[11520]{0:T(1024)S(1)} %scatter_fusion.4, s32[32768]{0:T(1024)S(1)} %bitcast.1641, f32[32768]{0:T(1024)S(1)} %copy-done.22), kind=kCustom, calls=%fused_computation.6 | custom fusion | flops 32768 | bytes 524288 | tf_op jit(solution)/shard_map/scatter-add | solution.py:171
  1275.9 174.7 %scatter_fusion.6 = f32[11520]{0:T(1024)S(1)} fusion(f32[11520]{0:T(1024)S(1)} %scatter_fusion.5, s32[32768]{0:T(1024)S(1)} %bitcast.1640, f32[32768]{0:T(1024)S(1)} %copy-done.21), kind=kCustom, calls=%fused_computation.7 | custom fusion | flops 32768 | bytes 524288 | tf_op jit(solution)/shard_map/scatter-add | solution.py:171
  1451.3 8.6 collective-permute-done
  1460.0 1.1 collective-permute-done.1
  1461.3 7.4 collective-permute-start.3
  1468.8 1.6 collective-permute-done.2
  1470.5 0.9 collective-permute-start.5
  1482.5 7.5 collective-permute-start.7
  1490.0 1.3 fusion.221
  1491.5 1.1 collective-permute-done.6
  1505.0 7.5 collective-permute-start.11
  1513.2 0.8 reshape.1248
  1519.5 1.8 rev.7
  1521.3 1.8 copy.302
  1523.0 1.0 reshape_reshape.7
  1524.1 1.8 rev.6
  1525.9 1.7 copy.296
  1527.6 1.0 reshape_reshape.6
  1531.1 1.0 pad_maximum_fusion.2
  1541.9 1.0 copy-done.1
  1544.8 1.8 collective-permute-start.15
  1552.1 4.6 collective-permute-done.14
  1558.9 0.9 copy.473
  1560.0 1.5 pad_maximum_fusion
  1574.0 2.7 collective-permute-start.19
  1581.8 4.8 collective-permute-done.18
  1603.2 3.9 all-reduce.1
  1607.1 344.1 %all-reduce = (f32[16,27]{0,1:T(8,128)S(1)}, f32[16,432]{1,0:T(8,128)S(1)}, f32[16,432]{1,0:T(8,128)S(1)}, f32[3,32]{1,0:T(4,128)S(1)}) all-reduce(f32[16,27]{0,1:T(8,128)S(1)} %get-tuple-element.48, f32[16,432]{1,0:T(8,128)S(1)} %get-tuple-element.49, ...), channel_id=1, replica_groups=mesh['slab'=64,'sub'=2] {'slab'}, use_global_device_ids=true, to_apply=%region_9.10 | all-reduce | flops 14352 | bytes 114816 | tf_op jit(solution)/shard_map/psum | solution.py:10
  (819 shorter events, 87.0 us)
Async XLA Ops:
  0.6 1489.4 %copy-start = (bf16[3,32]{1,0:T(4,128)(2,1)S(1)}, bf16[3,32]{1,0:T(4,128)(2,1)}, u32[]{:S(2)}) copy-start(bf16[3,32]{1,0:T(4,128)(2,1)} %param.18) | copy-start | bytes 580
  2.0 20.4 %all-to-all-start.1 = ((s32[1,128,1]{2,0,1:T(1,128)}), s32[1,128,1]{2,0,1:T(1,128)S(1)}, u32[]{:S(2)}, u32[]{:S(2)}) async-start(s32[1,128,1]{2,0,1:T(1,128)} %copy.241), calls=%async_computation.1 | async-start | bytes 131072 | tf_op jit(solution)/shard_map/all_to_all | solution.py:147
  22.5 14.2 all-to-all-start
  36.7 18.4 all-to-all-start.2
  401.9 174.9 %copy-start.20 = (s32[32768,1]{0,1:T(1,128)S(1)}, s32[32768,1]{0,1:T(1,128)}, u32[]{:S(2)}) copy-start(s32[32768,1]{0,1:T(1,128)} %get-tuple-element.371) | copy-start | bytes 393220
  401.9 174.9 %copy-start.25 = (f32[32768]{0:T(1024)S(1)}, f32[32768]{0:T(1024)}, u32[]{:S(2)}) copy-start(f32[32768]{0:T(1024)} %get-tuple-element.97) | copy-start | bytes 393220
  576.9 174.7 %copy-start.24 = (f32[32768]{0:T(1024)S(1)}, f32[32768]{0:T(1024)}, u32[]{:S(2)}) copy-start(f32[32768]{0:T(1024)} %get-tuple-element.94) | copy-start | bytes 393220
  576.9 174.7 %copy-start.26 = (s32[32768,1]{0,1:T(1,128)S(1)}, s32[32768,1]{0,1:T(1,128)}, u32[]{:S(2)}) copy-start(s32[32768,1]{0,1:T(1,128)} %get-tuple-element.223) | copy-start | bytes 393220
  751.7 174.7 %copy-start.19 = (s32[32768,1]{0,1:T(1,128)S(1)}, s32[32768,1]{0,1:T(1,128)}, u32[]{:S(2)}) copy-start(s32[32768,1]{0,1:T(1,128)} %get-tuple-element.222) | copy-start | bytes 393220
  751.7 174.7 %copy-start.23 = (f32[32768]{0:T(1024)S(1)}, f32[32768]{0:T(1024)}, u32[]{:S(2)}) copy-start(f32[32768]{0:T(1024)} %get-tuple-element.96) | copy-start | bytes 393220
  926.4 174.7 %copy-start.18 = (s32[32768,1]{0,1:T(1,128)S(1)}, s32[32768,1]{0,1:T(1,128)}, u32[]{:S(2)}) copy-start(s32[32768,1]{0,1:T(1,128)} %get-tuple-element.58) | copy-start | bytes 393220
  926.4 174.7 %copy-start.22 = (f32[32768]{0:T(1024)S(1)}, f32[32768]{0:T(1024)}, u32[]{:S(2)}) copy-start(f32[32768]{0:T(1024)} %get-tuple-element.95) | copy-start | bytes 393220
  1101.2 174.7 %copy-start.17 = (s32[32768,1]{0,1:T(1,128)S(1)}, s32[32768,1]{0,1:T(1,128)}, u32[]{:S(2)}) copy-start(s32[32768,1]{0,1:T(1,128)} %get-tuple-element.52) | copy-start | bytes 393220
  1101.2 174.7 %copy-start.21 = (f32[32768]{0:T(1024)S(1)}, f32[32768]{0:T(1024)}, u32[]{:S(2)}) copy-start(f32[32768]{0:T(1024)} %get-tuple-element.92) | copy-start | bytes 393220
  1275.9 195.4 %copy-start.69 = (bf16[16,27]{1,0:T(8,128)(2,1)S(1)}, bf16[16,27]{1,0:T(8,128)(2,1)}, u32[]{:S(2)}) copy-start(bf16[16,27]{1,0:T(8,128)(2,1)} %param.15) | copy-start | bytes 2596
  1275.9 195.5 %copy-start.67 = (bf16[3,4,8,256]{3,2,1,0:T(8,128)(2,1)S(1)}, bf16[3,4,8,256]{3,2,1,0:T(8,128)(2,1)}, u32[]{:S(2)}) copy-start(bf16[3,4,8,256]{3,2,1,0:T(8,128)(2,1)} %param.19) | copy-start | bytes 147460
  1450.7 9.2 collective-permute-start
  1459.9 1.2 collective-permute-start.1
  1461.2 9.1 collective-permute-start.2
  1461.3 9.0 collective-permute-start.3
  1470.4 1.2 collective-permute-start.4
  1470.5 1.7 collective-permute-start.5
  1473.2 8.5 copy-start.51
  1473.3 8.3 copy-start.53
  1473.3 8.0 copy-start.55
  1473.4 7.7 copy-start.37
  1473.4 7.5 copy-start.39
  1473.5 7.2 copy-start.41
  1482.2 9.1 copy-start.63
  1482.4 10.9 copy-start.65
  1482.4 10.1 collective-permute-start.6
  1482.5 10.0 collective-permute-start.7
  1492.6 1.3 collective-permute-start.8
  1492.7 1.4 collective-permute-start.9
  1503.2 9.9 copy-start.64
  1503.3 10.7 copy-start.66
  1505.0 23.7 %collective-permute-start.10 = (bf16[16,1,8,256]{3,0,2,1:T(8,128)(2,1)}, bf16[16,1,8,256]{3,0,2,1:T(8,128)(2,1)}, u32[]{:S(2)}, u32[]{:S(2)}) collective-permute-start(bf16[16,1,8,256]{3,0,2,1:T(8,128)(2,1)} %get-tuple-element.138), channel_id=1, source_target_pairs={{0,2},{2,4},{4,6},{6,8},{8,10},{10,12},{12,14},{14,16},{16,18},{18... | collective-permute-start | bytes 196616 | tf_op jit(solution)/shard_map/ppermute | solution.py:20
  1505.0 23.7 %collective-permute-start.11 = (bf16[16,1,8,256]{3,0,2,1:T(8,128)(2,1)}, bf16[16,1,8,256]{3,0,2,1:T(8,128)(2,1)}, u32[]{:S(2)}, u32[]{:S(2)}) collective-permute-start(bf16[16,1,8,256]{3,0,2,1:T(8,128)(2,1)} %get-tuple-element.139), channel_id=1, source_target_pairs={{2,0},{4,2},{6,4},{8,6},{10,8},{12,10},{14,12},{16,14},{18,16},{20... | collective-permute-start | bytes 196616 | tf_op jit(solution)/shard_map/ppermute | solution.py:21
  1529.5 1.3 collective-permute-start.12
  1529.6 1.5 collective-permute-start.13
  1544.8 11.9 collective-permute-start.15
  1546.9 9.8 collective-permute-start.14
  1557.5 2.4 collective-permute-start.16
  1557.5 2.4 collective-permute-start.17
  1574.0 7.7 collective-permute-start.19
  1576.8 9.8 collective-permute-start.18
  1586.6 1.3 collective-permute-start.20
  1586.7 1.6 collective-permute-start.21
  (47 other events, 91.0 us)
